TPU v7x, 32 devices: a whole 2x2x4 slice. The times are simulated.
32 devices in a mesh: layer: 4 (over x, core), dp: 8 (over z, y).
Axes of the slice: x: 2, y: 2, z: 4, core: 2. Of those that a mesh axis runs over, the one named last changes fastest.
Arguments:
- out_grads: bfloat16 [4, 128, 16384], P('layer', None, 'dp'), may hold values from -3 to 3
- in_acts: bfloat16 [4, 128, 4096], P('layer', None, 'dp'), may hold values from -3 to 3
- out_basis: bfloat16 [4, 16384, 16384], P('layer', None, 'dp'), may hold values from -0.046875 to 0.046875
- in_basis: bfloat16 [4, 4096, 4096], P('layer', None, 'dp'), may hold values from -0.09375 to 0.09375
- eigenvalues: bfloat16 [4, 16384, 4096], P('layer', 'dp'), may hold values from 0.5 to 50
- out_store: bfloat16 [4, 16, 32, 16384], P('layer', 'dp'), may hold values from -0.046875 to 0.046875
- in_store: bfloat16 [4, 16, 32, 4096], P('layer', 'dp'), may hold values from -0.09375 to 0.09375
- counts: int32 [16], P('dp'), may hold values from 1 to 4096
- winners: int32 [4, 6], replicated, may hold values from 0 to 15
Outputs:
- influence: float32 [4, 6, 32], replicated
All inputs are finite; a program needn't handle non-finite values.
Results may differ from a plain program's by a relative error of at most 0.0055.
Values may be sent and summed in bfloat16 or wider, within the bound.
A program may use at most 192 MiB of HBM per device.

v0:
```python
import jax
import jax.numpy as jnp
from jax import lax
from jax.sharding import PartitionSpec as P

NQ = 4
TQ = 32
WIN = 6
R = 32
SPAN = 128
damping = 0.1


def on_device(
    out_grads, in_acts, out_basis, in_basis, eigenvalues, out_store, in_store, counts, winners
):
    out_local = out_basis[0]
    in_local = in_basis[0]
    out_width = out_local.shape[1]
    rows = out_local
    turned_out = jnp.dot(
        lax.all_gather(out_grads[0], "dp", axis=1, tiled=True),
        rows,
        preferred_element_type=jnp.float32,
    ).astype(jnp.bfloat16)
    rows = in_local
    turned_part = jnp.dot(
        lax.all_gather(in_acts[0], "dp", axis=1, tiled=True),
        rows,
        preferred_element_type=jnp.float32,
    ).astype(jnp.bfloat16)
    turned_in = lax.all_gather(turned_part, "dp", axis=1, tiled=True)
    left = turned_out.reshape(NQ, TQ, out_width)
    right = turned_in.reshape(NQ, TQ, turned_in.shape[1])
    product = jnp.einsum("qtf,qtd->qfd", left, right, preferred_element_type=jnp.float32)
    divisor = eigenvalues[0].astype(jnp.float32) + damping
    precond = (product / divisor[None]).astype(jnp.bfloat16)
    alive = (jnp.arange(R, dtype=jnp.int32)[None, :] * SPAN < counts[:, None]).astype(jnp.bfloat16)
    masked = in_store[0] * alive[:, :, None]
    out_slices = lax.all_to_all(out_store[0], "dp", split_axis=2, concat_axis=0, tiled=True)
    chosen = winners.reshape(NQ * WIN)
    left_rows = jnp.take(out_slices, chosen, axis=0).reshape(NQ, WIN * R, out_width)
    full_width = turned_in.shape[1]
    in_whole = lax.all_gather(masked, "dp", axis=0, tiled=True)
    right_rows = jnp.take(in_whole, chosen, axis=0).reshape(NQ, WIN * R, full_width)
    mapped = jnp.einsum("qfd,qkd->qkf", precond, right_rows, preferred_element_type=jnp.float32)
    partial_value = jnp.sum(mapped * left_rows.astype(jnp.float32), axis=2)
    totals = lax.psum(partial_value, ("layer", "dp"))
    return totals.reshape(NQ, WIN, R)


def solution(mesh):
    placed = (
        P("layer", None, "dp"),
        P("layer", None, "dp"),
        P("layer", None, "dp"),
        P("layer", None, "dp"),
        P("layer", "dp", None),
        P("layer", "dp", None, None),
        P("layer", "dp", None, None),
        P("dp"),
        P(),
    )
    return jax.shard_map(on_device, mesh=mesh, in_specs=placed, out_specs=P(), check_vma=False)
```

profile of v0, /device:TPU:0, one launch (start us, length us, event | category | flops | bytes accessed | tf_op | source)
XLA Modules:
  0.0 364.3 jit_solution(16281501123913025915)
XLA Ops:
  6.5 0.7 all-gather.13.cloned.1.call-update
  7.3 0.0 all-gather.11.cloned.1.call-start
  7.3 0.7 all-gather.11.cloned.1.call-update
  8.0 0.0 all-gather.7.cloned.1.call-start
  8.1 0.7 compare_convert_fusion
  8.8 2.0 bitcast_multiply_fusion
  10.7 0.0 all-gather.7.cloned.1.call-update
  10.8 17.2 %copy.13 = bf16[1,2,32,16384]{2,1,3,0:T(2,128)(2,1)} copy(bf16[1,2,32,16384]{3,2,1,0:T(8,128)(2,1)} %param.14) | data formatting | bytes 4194304 | tf_op args[5]
  28.0 8.0 %bitcast_bitcast_fusion = bf16[16384,2,32]{2,1,0:T(2,128)(2,1)} fusion(bf16[1,2,32,16384]{2,1,3,0:T(2,128)(2,1)} %copy.13), kind=kLoop, calls=%fused_computation.25 | loop fusion | bytes 4194304
  36.0 11.2 %reshape.112 = bf16[8,2,65536]{2,1,0:T(2,128)(2,1)} reshape(bf16[16384,2,32]{2,1,0:T(2,128)(2,1)} %bitcast_bitcast_fusion) | data formatting | bytes 4194304
  47.2 7.3 %all-to-all-start = ((bf16[8,2,65536]{2,1,0:T(2,128)(2,1)}), bf16[8,2,65536]{2,1,0:T(2,128)(2,1)S(1)}, u32[]{:S(2)}, u32[]{:S(2)}) async-start(bf16[8,2,65536]{2,1,0:T(2,128)(2,1)} %reshape.112), calls=%async_computation | async-start | bytes 4194304 | tf_op jit(solution)/shard_map/all_to_all | solution.py:40
  54.5 0.0 all-gather.9.cloned.1.call-start
  54.6 0.1 reshape.90
  54.7 0.1 broadcast_in_dim.28
  54.8 0.1 broadcast_in_dim.29
  54.9 18.8 %add_bitcast_fusion = f32[2048,4096]{1,0:T(8,128)} fusion(bf16[1,2048,4096]{2,1,0:T(8,128)(2,1)} %param.13), kind=kLoop, calls=%fused_computation.6 | loop fusion | flops 16777216 | bytes 50331648 | tf_op jit(solution)/shard_map/div | solution.py:37
  73.7 3.9 %fusion.13 = bf16[128,512]{1,0:T(8,128)(2,1)} fusion(bf16[1,4096,512]{2,1,0:T(8,128)(2,1)} %param.12, bf16[1,128,4096]{2,1,0:T(8,128)(2,1)} %all-gather.13.cloned.1.call-done), kind=kOutput, calls=%fused_computation.15 | convolution fusion | flops 536936448 | bytes 5373952 | tf_op jit(solution)/shard_map/dot_general | solution.py:27
  77.6 0.0 all-gather.9.cloned.1.call-update
  77.6 50.9 %all-to-all-done = bf16[8,2,65536]{2,1,0:T(2,128)(2,1)S(1)} async-done(((bf16[8,2,65536]{2,1,0:T(2,128)(2,1)}), bf16[8,2,65536]{2,1,0:T(2,128)(2,1)S(1)}, u32[]{:S(2)}, u32[]{:S(2)}) %all-to-all-start) | async-done | bytes 2097184 | tf_op jit(solution)/shard_map/all_to_all | solution.py:40
  128.5 6.5 %reshape.113 = bf16[16384,2,32]{2,1,0:T(2,128)(2,1)} reshape(bf16[8,2,65536]{2,1,0:T(2,128)(2,1)S(1)} %all-to-all-done) | data formatting | bytes 4194304
  135.0 17.8 %copy.18 = bf16[2,32,8,2048]{3,1,0,2:T(8,128)(2,1)S(1)} copy(bf16[2,32,8,2048]{1,0,3,2:T(2,128)(2,1)} %bitcast.47) | data formatting | bytes 4194304 | tf_op jit(solution)/shard_map/all_to_all | solution.py:40
  152.8 2.5 gather_fusion.1
  155.3 26.3 %fusion.8 = bf16[128,2048]{1,0:T(8,128)(2,1)} fusion(bf16[1,16384,2048]{2,1,0:T(8,128)(2,1)} %param.11, bf16[1,128,16384]{2,1,0:T(8,128)(2,1)} %all-gather.11.cloned.1.call-done), kind=kOutput, calls=%fused_computation.14 | convolution fusion | flops 8590196736 | bytes 71827456 | tf_op jit(solution)/shard_map/dot_general | solution.py:21
  181.5 46.3 %all-gather.7.cloned.1.call-done = bf16[16,32,4096]{2,1,0:T(8,128)(2,1)} async-done(((bf16[2,32,4096]{2,1,0:T(8,128)(2,1)}), bf16[16,32,4096]{2,1,0:T(8,128)(2,1)}) %all-gather.7.cloned.1.call-update) | async-done | bytes 4194320 | tf_op jit(solution)/shard_map/all_gather | solution.py:44
  227.8 6.5 %gather_fusion = bf16[24,32,4096]{2,1,0:T(8,128)(2,1)} fusion(bf16[16,32,4096]{2,1,0:T(8,128)(2,1)} %all-gather.7.cloned.1.call-done, s32[1024]{0:T(1024)S(1)} %pad_clamp_fusion), kind=kCustom, calls=%fused_computation | custom fusion | bytes 12583008 | tf_op jit(solution)/shard_map/jit(_take)/gather | solution.py:45
  234.3 6.1 %bitcast_select_fusion = bf16[4,192,4096]{2,1,0:T(8,128)(2,1)} fusion(pred[4,192]{1,0:T(4,128)(4,1)S(1)} %broadcast_in_dim.29, bf16[4,192,4096]{2,1,0:T(8,128)(2,1)} %bitcast.48), kind=kLoop, calls=%fused_computation.8 | loop fusion | flops 3145728 | bytes 12583680 | tf_op jit(solution)/shard_map/jit(_take)/select_n | solution.py:45
  240.5 27.2 %all-gather.9.cloned.1.call-done = bf16[128,4096]{1,0:T(8,128)(2,1)} async-done(((bf16[128,512]{1,0:T(8,128)(2,1)}), bf16[128,4096]{1,0:T(8,128)(2,1)}) %all-gather.9.cloned.1.call-update) | async-done | bytes 1048592 | tf_op jit(solution)/shard_map/all_gather | solution.py:32
  267.7 45.8 %fusion.2 = f32[4,192,2048]{2,1,0:T(8,128)} fusion(bf16[4,192,4096]{2,1,0:T(8,128)(2,1)} %bitcast_select_fusion, f32[2048,4096]{1,0:T(8,128)} %add_bitcast_fusion, bf16[4,32,2048]{2,1,0:T(8,128)(2,1)} %bitcast.51, bf16[4,32,4096]{2,1,0:T(8,128)(2,1)} %bitcast.52), kind=kOutput, calls=%fused_computation.5 | convolution fusion | flops 15099494400 | bytes 47710208 | tf_op jit(solution)/shard_map/qfd,qkd->qkf/dot_general | solution.py:46
  313.5 3.8 %multiply_reduce_fusion = f32[4,192]{1,0:T(4,128)S(1)} fusion(f32[4,192,2048]{2,1,0:T(8,128)} %fusion.2, pred[4,192]{1,0:T(4,128)(4,1)S(1)} %broadcast_in_dim.29, bf16[4,192,2048]{2,1,0:T(8,128)(2,1)S(1)} %bitcast.50), kind=kLoop, calls=%fused_computation.9 | loop fusion | flops 6290688 | bytes 9441024 | tf_op jit(solution)/shard_map/reduce_sum | solution.py:47
  317.3 0.1 reshape.93
  317.4 39.8 %psum.7 = f32[4,6,32]{2,1,0:T(8,128)S(1)} all-reduce(f32[4,6,32]{2,1,0:T(8,128)S(1)} %reshape.93), channel_id=1, replica_groups=mesh['layer'=4,'dp'=8] {'layer','dp'}, use_global_device_ids=true, to_apply=%region_1.2 | all-reduce | flops 768 | bytes 6144 | tf_op jit(solution)/shard_map/psum | solution.py:48
  357.2 0.6 copy.16
  (11 shorter events, 0.0 us)
Async XLA Ops:
  6.5 67.1 %all-gather.13.cloned.1.call-start = ((), (), s32[]{:S(2)}) async-start(), calls=%async_computation.4 | async-start | bytes 1179648 | tf_op jit(solution)/shard_map/all_gather | solution.py:28
  7.3 148.0 %all-gather.11.cloned.1.call-start = ((), (), s32[]{:S(2)}) async-start(), calls=%async_computation.3 | async-start | bytes 4718592 | tf_op jit(solution)/shard_map/all_gather | solution.py:22
  8.0 219.8 %all-gather.7.cloned.1.call-start = ((), (), s32[]{:S(2)}) async-start(), calls=%async_computation.1 | async-start | bytes 4718592 | tf_op jit(solution)/shard_map/all_gather | solution.py:44
  36.0 18.6 %copy-start.1 = (s32[4,6]{1,0:T(4,128)S(1)}, s32[4,6]{1,0:T(4,128)}, u32[]{:S(2)}) copy-start(s32[4,6]{1,0:T(4,128)} %param.17) | copy-start | bytes 292
  47.2 81.3 %all-to-all-start = ((bf16[8,2,65536]{2,1,0:T(2,128)(2,1)}), bf16[8,2,65536]{2,1,0:T(2,128)(2,1)S(1)}, u32[]{:S(2)}, u32[]{:S(2)}) async-start(bf16[8,2,65536]{2,1,0:T(2,128)(2,1)} %reshape.112), calls=%async_computation | async-start | bytes 4194304 | tf_op jit(solution)/shard_map/all_to_all | solution.py:40
  54.5 213.1 %all-gather.9.cloned.1.call-start = ((), (), s32[]{:S(2)}) async-start(), calls=%async_computation.2 | async-start | bytes 1179648 | tf_op jit(solution)/shard_map/all_gather | solution.py:32
  267.7 45.8 %copy-start = (bf16[24,32,2048]{2,1,0:T(8,128)(2,1)S(1)}, bf16[24,32,2048]{2,1,0:T(8,128)(2,1)}, u32[]{:S(2)}) copy-start(bf16[24,32,2048]{2,1,0:T(8,128)(2,1)} %gather_fusion.1) | copy-start | bytes 9437188
Sparse Core Ops, SparseCore 0:
  9.4 42.1 all-gather.12
  53.7 100.1 all-gather.10
  156.0 71.7 all-gather.6
  229.7 37.9 all-gather.8
where the time goes:
time: 366 us; the launch traced here: 364 us
  waiting for transfers between devices  126 us (34%)
  matrix products  76 us (21%)
  local copies, waits for them, and re-layouts  70.7 us (19%)
  blocking collectives  39.8 us (11%)
  other arithmetic  31.4 us (9%)
  between operations  13.2 us (4%)
  starting transfers between devices  7.43 us (2%)
    all_to_all x1, waiting for transfers between devices, on_device(): lax.all_to_all(out_store[0], 'dp', split_axis=2, concat_axis=0, tiled=True)  50.9 us
    all_gather x1, waiting for transfers between devices, on_device(): in_whole = lax.all_gather(masked, 'dp', axis=0, tiled=True)  46.3 us
    dot_general x1, matrix products, on_device(): jnp.einsum('qfd,qkd->qkf', precond, right_rows, preferred_element_type=jn...  45.8 us
    unnamed x8, local copies, waits for them, and re-layouts  43 us
    psum x1, blocking collectives, on_device(): totals = lax.psum(partial_value, ('layer', 'dp'))  39.8 us
    all_gather x1, waiting for transfers between devices, on_device(): turned_in = lax.all_gather(turned_part, 'dp', axis=1, tiled=True)  27.2 us
    dot_general x1, matrix products, on_device(): jnp.dot(lax.all_gather(out_grads[0], 'dp', axis=1, tiled=True), rows, pre...  26.3 us
    div x1, other arithmetic, on_device(): precond = (product / divisor[None]).astype(jnp.bfloat16)  18.8 us
  transfers between devices with their start and end apart: 5, of which 3 were waited for; matrix products, arithmetic and copies ran while one was open for 35% of the time, Pallas kernels for 0%

commit v1 on v0

--- a/solution.py
+++ b/solution.py
@@ -37,7 +37,10 @@
     precond = (product / divisor[None]).astype(jnp.bfloat16)
     alive = (jnp.arange(R, dtype=jnp.int32)[None, :] * SPAN < counts[:, None]).astype(jnp.bfloat16)
     masked = in_store[0] * alive[:, :, None]
-    out_slices = lax.all_to_all(out_store[0], "dp", split_axis=2, concat_axis=0, tiled=True)
+    out_slices = jnp.concatenate(
+        lax.all_to_all(jnp.stack(jnp.split(out_store[0], lax.axis_size("dp"), axis=2)), "dp", 0, 0),
+        axis=0,
+    )
     chosen = winners.reshape(NQ * WIN)
     left_rows = jnp.take(out_slices, chosen, axis=0).reshape(NQ, WIN * R, out_width)
     full_width = turned_in.shape[1]

time: 366 us -> 367 us (level)
  waiting for transfers between devices: 126 us -> 181 us
  local copies, waits for them, and re-layouts: 70.7 us -> 17.6 us
    all_gather x1, waiting for transfers between devices: 0.01 us -> 69.3 us  [on_device(): lax.all_gather(out_grads[0], 'dp', axis=1, tiled=True)]
    all_to_all x1, waiting for transfers between devices: 50.9 us -> 2.02 us  [on_device(): lax.all_to_all(jnp.stack(jnp.split(out_store[0], lax.axis_size('dp'), axi...]
    unnamed x8 -> x13, local copies, waits for them, and re-layouts: 43 us -> 6.98 us
    all_gather x1, waiting for transfers between devices: 0.01 us -> 33.5 us  [on_device(): lax.all_gather(in_acts[0], 'dp', axis=1, tiled=True)]
    all_to_all x1 -> x0, local copies, waits for them, and re-layouts: 17.8 us -> none  [on_device(): lax.all_to_all(out_store[0], 'dp', split_axis=2, concat_axis=0, tiled=True)]
  transfers between devices with their start and end apart: 5 -> 5, of which waited for: 3 -> 5; matrix products, arithmetic and copies ran while one was open for 35% -> 20% of each run, Pallas kernels for 0% -> 0%
where the time goes in v1:
time: 367 us; the launch traced here: 366 us
  waiting for transfers between devices  181 us (49%)
  matrix products  75.9 us (21%)
  blocking collectives  39.9 us (11%)
  other arithmetic  31.3 us (9%)
  local copies, waits for them, and re-layouts  17.6 us (5%)
  between operations  13.2 us (4%)
  starting transfers between devices  7.42 us (2%)
    all_gather x1, waiting for transfers between devices, on_device(): lax.all_gather(out_grads[0], 'dp', axis=1, tiled=True)  69.3 us
    all_gather x1, waiting for transfers between devices, on_device(): in_whole = lax.all_gather(masked, 'dp', axis=0, tiled=True)  47.2 us
    dot_general x1, matrix products, on_device(): jnp.einsum('qfd,qkd->qkf', precond, right_rows, preferred_element_type=jn...  45.8 us
    psum x1, blocking collectives, on_device(): totals = lax.psum(partial_value, ('layer', 'dp'))  39.9 us
    all_gather x1, waiting for transfers between devices, on_device(): lax.all_gather(in_acts[0], 'dp', axis=1, tiled=True)  33.5 us
    all_gather x1, waiting for transfers between devices, on_device(): turned_in = lax.all_gather(turned_part, 'dp', axis=1, tiled=True)  27.2 us
    dot_general x1, matrix products, on_device(): jnp.dot(lax.all_gather(out_grads[0], 'dp', axis=1, tiled=True), rows, pre...  26.2 us
    div x1, other arithmetic, on_device(): precond = (product / divisor[None]).astype(jnp.bfloat16)  18.7 us
  transfers between devices with their start and end apart: 5, of which 5 were waited for; matrix products, arithmetic and copies ran while one was open for 20% of the time, Pallas kernels for 0%

profile of v1, /device:TPU:0, one launch (start us, length us, event | category | flops | bytes accessed | tf_op | source)
XLA Modules:
  0.0 366.0 jit_solution(10151527656305338172)
XLA Ops:
  6.5 0.7 all-gather.13.cloned.1.call-update
  7.3 0.7 all-gather.11.cloned.1.call-update
  8.1 0.7 compare_convert_fusion
  8.8 1.9 bitcast_multiply_fusion
  10.8 1.7 fusion.24
  12.4 1.7 fusion.23
  14.1 0.7 fusion.22
  14.8 0.7 fusion.21
  15.5 0.7 fusion.20
  16.3 0.7 fusion.19
  17.0 0.7 fusion.18
  17.7 0.7 fusion.17
  18.5 7.3 %all-to-all-start = ((bf16[8,2,32,2048]{3,2,1,0:T(8,128)(2,1)}), bf16[8,2,32,2048]{3,2,1,0:T(8,128)(2,1)S(1)}, u32[]{:S(2)}, u32[]{:S(2)}) async-start(bf16[8,2,32,2048]{3,2,1,0:T(8,128)(2,1)} %fusion.17), calls=%async_computation | async-start | bytes 4194304 | tf_op jit(solution)/shard_map/all_to_all | solution.py:41
  25.8 0.1 reshape.93
  25.9 0.1 broadcast_in_dim.28
  26.0 0.1 broadcast_in_dim.29
  26.1 18.7 %add_bitcast_fusion = f32[2048,4096]{1,0:T(8,128)} fusion(bf16[1,2048,4096]{2,1,0:T(8,128)(2,1)} %param.13), kind=kLoop, calls=%fused_computation.6 | loop fusion | flops 16777216 | bytes 50331648 | tf_op jit(solution)/shard_map/div | solution.py:37
  44.8 33.5 %all-gather.13.cloned.1.call-done = bf16[1,128,4096]{2,1,0:T(8,128)(2,1)} async-done(((bf16[1,128,512]{2,1,0:T(8,128)(2,1)}), bf16[1,128,4096]{2,1,0:T(8,128)(2,1)}) %all-gather.13.cloned.1.call-update) | async-done | bytes 1048592 | tf_op jit(solution)/shard_map/all_gather | solution.py:28
  78.3 3.9 %fusion.13 = bf16[128,512]{1,0:T(8,128)(2,1)} fusion(bf16[1,4096,512]{2,1,0:T(8,128)(2,1)} %param.12, bf16[1,128,4096]{2,1,0:T(8,128)(2,1)} %all-gather.13.cloned.1.call-done), kind=kOutput, calls=%fused_computation.15 | convolution fusion | flops 536936448 | bytes 5373952 | tf_op jit(solution)/shard_map/dot_general | solution.py:27
  82.2 2.0 all-to-all-done
  84.2 2.5 gather_fusion.1
  86.7 69.3 %all-gather.11.cloned.1.call-done = bf16[1,128,16384]{2,1,0:T(8,128)(2,1)} async-done(((bf16[1,128,2048]{2,1,0:T(8,128)(2,1)}), bf16[1,128,16384]{2,1,0:T(8,128)(2,1)}) %all-gather.11.cloned.1.call-update) | async-done | bytes 4194320 | tf_op jit(solution)/shard_map/all_gather | solution.py:22
  156.0 26.2 %fusion.8 = bf16[128,2048]{1,0:T(8,128)(2,1)} fusion(bf16[1,16384,2048]{2,1,0:T(8,128)(2,1)} %param.11, bf16[1,128,16384]{2,1,0:T(8,128)(2,1)} %all-gather.11.cloned.1.call-done), kind=kOutput, calls=%fused_computation.14 | convolution fusion | flops 8590196736 | bytes 71827456 | tf_op jit(solution)/shard_map/dot_general | solution.py:21
  182.3 47.2 %all-gather.7.cloned.1.call-done = bf16[16,32,4096]{2,1,0:T(8,128)(2,1)} async-done(((bf16[2,32,4096]{2,1,0:T(8,128)(2,1)}), bf16[16,32,4096]{2,1,0:T(8,128)(2,1)}) %all-gather.7.cloned.1.call-update) | async-done | bytes 4194320 | tf_op jit(solution)/shard_map/all_gather | solution.py:47
  229.5 6.5 %gather_fusion = bf16[24,32,4096]{2,1,0:T(8,128)(2,1)} fusion(bf16[16,32,4096]{2,1,0:T(8,128)(2,1)} %all-gather.7.cloned.1.call-done, s32[1024]{0:T(1024)S(1)} %pad_clamp_fusion), kind=kCustom, calls=%fused_computation | custom fusion | bytes 12583008 | tf_op jit(solution)/shard_map/jit(_take)/gather | solution.py:48
  236.0 6.1 %bitcast_select_fusion = bf16[4,192,4096]{2,1,0:T(8,128)(2,1)} fusion(pred[4,192]{1,0:T(4,128)(4,1)S(1)} %broadcast_in_dim.29, bf16[4,192,4096]{2,1,0:T(8,128)(2,1)} %bitcast.71), kind=kLoop, calls=%fused_computation.8 | loop fusion | flops 3145728 | bytes 12583680 | tf_op jit(solution)/shard_map/jit(_take)/select_n | solution.py:48
  242.1 27.2 %all-gather.9.cloned.1.call-done = bf16[128,4096]{1,0:T(8,128)(2,1)} async-done(((bf16[128,512]{1,0:T(8,128)(2,1)}), bf16[128,4096]{1,0:T(8,128)(2,1)}) %all-gather.9.cloned.1.call-update) | async-done | bytes 1048592 | tf_op jit(solution)/shard_map/all_gather | solution.py:32
  269.4 45.8 %fusion.2 = f32[4,192,2048]{2,1,0:T(8,128)} fusion(bf16[4,192,4096]{2,1,0:T(8,128)(2,1)} %bitcast_select_fusion, f32[2048,4096]{1,0:T(8,128)} %add_bitcast_fusion, bf16[4,32,2048]{2,1,0:T(8,128)(2,1)} %bitcast.82, bf16[4,32,4096]{2,1,0:T(8,128)(2,1)} %bitcast.83), kind=kOutput, calls=%fused_computation.5 | convolution fusion | flops 15099494400 | bytes 47710208 | tf_op jit(solution)/shard_map/qfd,qkd->qkf/dot_general | solution.py:49
  315.2 3.8 %multiply_reduce_fusion = f32[4,192]{1,0:T(4,128)S(1)} fusion(f32[4,192,2048]{2,1,0:T(8,128)} %fusion.2, pred[4,192]{1,0:T(4,128)(4,1)S(1)} %broadcast_in_dim.29, bf16[4,192,2048]{2,1,0:T(8,128)(2,1)S(1)} %bitcast.73), kind=kLoop, calls=%fused_computation.9 | loop fusion | flops 6290688 | bytes 9441024 | tf_op jit(solution)/shard_map/reduce_sum | solution.py:50
  318.9 0.1 reshape.97
  319.0 39.9 %psum.7 = f32[4,6,32]{2,1,0:T(8,128)S(1)} all-reduce(f32[4,6,32]{2,1,0:T(8,128)S(1)} %reshape.97), channel_id=1, replica_groups=mesh['layer'=4,'dp'=8] {'layer','dp'}, use_global_device_ids=true, to_apply=%region_1.2 | all-reduce | flops 768 | bytes 6144 | tf_op jit(solution)/shard_map/psum | solution.py:51
  358.9 0.6 copy.11
  (16 shorter events, 0.2 us)
Async XLA Ops:
  6.5 7.6 %copy-start.1 = (bf16[1,2,32,16384]{3,2,1,0:T(8,128)(2,1)S(1)}, bf16[1,2,32,16384]{3,2,1,0:T(8,128)(2,1)}, u32[]{:S(2)}) copy-start(bf16[1,2,32,16384]{3,2,1,0:T(8,128)(2,1)} %param.14) | copy-start | bytes 6291460
  6.5 71.7 %all-gather.13.cloned.1.call-start = ((), (), s32[]{:S(2)}) async-start(), calls=%async_computation.4 | async-start | bytes 1179648 | tf_op jit(solution)/shard_map/all_gather | solution.py:28
  7.3 148.7 %all-gather.11.cloned.1.call-start = ((), (), s32[]{:S(2)}) async-start(), calls=%async_computation.3 | async-start | bytes 4718592 | tf_op jit(solution)/shard_map/all_gather | solution.py:22
  8.0 221.5 %all-gather.7.cloned.1.call-start = ((), (), s32[]{:S(2)}) async-start(), calls=%async_computation.1 | async-start | bytes 4718592 | tf_op jit(solution)/shard_map/all_gather | solution.py:47
  15.5 10.3 %copy-start.2 = (s32[4,6]{1,0:T(4,128)S(1)}, s32[4,6]{1,0:T(4,128)}, u32[]{:S(2)}) copy-start(s32[4,6]{1,0:T(4,128)} %param.17) | copy-start | bytes 292
  18.5 65.8 %all-to-all-start = ((bf16[8,2,32,2048]{3,2,1,0:T(8,128)(2,1)}), bf16[8,2,32,2048]{3,2,1,0:T(8,128)(2,1)S(1)}, u32[]{:S(2)}, u32[]{:S(2)}) async-start(bf16[8,2,32,2048]{3,2,1,0:T(8,128)(2,1)} %fusion.17), calls=%async_computation | async-start | bytes 4194304 | tf_op jit(solution)/shard_map/all_to_all | solution.py:41
  25.8 243.6 %all-gather.9.cloned.1.call-start = ((), (), s32[]{:S(2)}) async-start(), calls=%async_computation.2 | async-start | bytes 1179648 | tf_op jit(solution)/shard_map/all_gather | solution.py:32
  269.4 45.8 %copy-start = (bf16[24,32,2048]{2,1,0:T(8,128)(2,1)S(1)}, bf16[24,32,2048]{2,1,0:T(8,128)(2,1)}, u32[]{:S(2)}) copy-start(bf16[24,32,2048]{2,1,0:T(8,128)(2,1)} %gather_fusion.1) | copy-start | bytes 9437188
Sparse Core Ops, SparseCore 0:
  9.4 68.8 all-gather.12
  80.5 75.4 all-gather.10
  158.1 71.3 all-gather.6
  231.4 37.9 all-gather.8
